TPU v7x, 128 devices: a whole 4x4x4 slice. The times are simulated.
128 devices in a mesh: sa: 4 (over x), sb: 2 (over core), sc: 16 (over z, y).
Axes of the slice: x: 4, y: 4, z: 4, core: 2. Of those that a mesh axis runs over, the one named last changes fastest.
Arguments:
- queries: float32 [65536, 2048], P(('sa', 'sb', 'sc')), may hold values from -6 to 6
- key_rows: float32 [65536, 2048], P(('sa', 'sb', 'sc')), may hold values from -6 to 6
- value_rows: float32 [65536, 2048], P(('sa', 'sb', 'sc')), may hold values from -6 to 6
- out_grad: float32 [65536, 2048], P(('sa', 'sb', 'sc')), may hold values from -6 to 6
- prefix_state: float32 [16, 128, 128], replicated, may hold values from -1536 to 1536
- suffix_state: float32 [16, 128, 128], replicated, may hold values from -1536 to 1536
Outputs:
- query_grad: bfloat16 [65536, 2048], P(('sa', 'sb', 'sc'))
- key_grad: bfloat16 [65536, 2048], P(('sa', 'sb', 'sc'))
- value_grad: bfloat16 [65536, 2048], P(('sa', 'sb', 'sc'))
All inputs are finite; a program needn't handle non-finite values.
Results may differ from a plain program's by a relative error of at most 0.0019.
Values sent between devices are 32-bit elements; how exact they have to be, the bound alone decides.
A program may use at most 576 MiB of HBM per device.

v0:
```python
import math
import jax
import jax.numpy as jnp
from jax import lax
from jax.sharding import PartitionSpec as P


def entering(part, axis, combine, identity):
    place = lax.axis_index(axis)
    gathered = jax.tree.map(lambda a: lax.all_gather(a, axis), part)
    state = jax.tree.map(lambda a, e: jnp.zeros_like(a) + jnp.asarray(e, a.dtype), part, identity)

    def one(hop, state):
        return combine(
            state, jax.tree.map(lambda a: lax.dynamic_index_in_dim(a, hop, 0, False), gathered)
        )

    return lax.fori_loop(0, place, one, state)


def add_states(earlier, later):
    return jax.tree.map(lambda left, right: left + right, earlier, later)


def run_chain(local_terms):
    zero_state = jax.tree.map(jnp.zeros_like, local_terms)
    inner_part = entering(local_terms, "sc", add_states, zero_state)
    group_sum = lax.psum((local_terms[0], local_terms[1]), "sc")
    middle_part = entering(group_sum, "sb", add_states, zero_state)
    block_sum = lax.psum((group_sum[0], group_sum[1]), "sb")
    outer_part = entering(block_sum, "sa", add_states, zero_state)
    return add_states(add_states(outer_part, middle_part), inner_part)


def shards(queries, key_rows, value_rows, out_grad, prefix_state, suffix_state):
    row_count = queries.shape[0]
    head_count = prefix_state.shape[0]
    head_size = prefix_state.shape[1]
    device_count = lax.axis_size("sa") * lax.axis_size("sb") * lax.axis_size("sc")
    factor = 1.0 / math.sqrt(head_size * row_count * device_count)
    highest = lax.Precision.HIGHEST
    shaped = (row_count, head_count, head_size)
    query_t = queries.reshape(shaped)
    key_t = key_rows.reshape(shaped)
    value_t = value_rows.reshape(shaped)
    grad_t = out_grad.reshape(shaped)
    kv_local = jnp.einsum("thd,the->hde", key_t, value_t, precision=highest)
    grad_local = jnp.einsum("the,thd->hed", grad_t, query_t, precision=highest)
    prior_kv, prior_grad = run_chain((kv_local, grad_local))
    total_grad = lax.psum(grad_local, ("sa", "sb", "sc"))
    state_before = prefix_state + prior_kv
    state_after = suffix_state + (total_grad - prior_grad - grad_local)
    lower = (
        lax.broadcasted_iota(jnp.int32, (row_count, row_count), 0)
        >= lax.broadcasted_iota(jnp.int32, (row_count, row_count), 1)
    ).astype(jnp.float32)
    grad_scores = jnp.einsum("the,she->hts", grad_t, value_t, precision=highest) * lower
    attn_scores = jnp.einsum("thd,shd->hts", query_t, key_t, precision=highest) * lower
    query_grad = factor * (
        jnp.einsum("the,hde->thd", grad_t, state_before, precision=highest)
        + jnp.einsum("hts,shd->thd", grad_scores, key_t, precision=highest)
    )
    key_grad = factor * (
        jnp.einsum("she,hed->shd", value_t, state_after, precision=highest)
        + jnp.einsum("hts,thd->shd", grad_scores, query_t, precision=highest)
    )
    value_grad = factor * (
        jnp.einsum("shd,hed->she", key_t, state_after, precision=highest)
        + jnp.einsum("hts,the->she", attn_scores, grad_t, precision=highest)
    )
    flat = (row_count, head_count * head_size)
    return (
        query_grad.astype(jnp.bfloat16).reshape(flat),
        key_grad.astype(jnp.bfloat16).reshape(flat),
        value_grad.astype(jnp.bfloat16).reshape(flat),
    )


def solution(mesh):
    return jax.shard_map(
        shards,
        mesh=mesh,
        in_specs=(
            P(("sa", "sb", "sc"), None),
            P(("sa", "sb", "sc"), None),
            P(("sa", "sb", "sc"), None),
            P(("sa", "sb", "sc"), None),
            P(),
            P(),
        ),
        out_specs=(
            P(("sa", "sb", "sc"), None),
            P(("sa", "sb", "sc"), None),
            P(("sa", "sb", "sc"), None),
        ),
        check_vma=False,
    )
```

profile of v0, /device:TPU:1, one launch (start us, length us, event | category | flops | bytes accessed | tf_op | source)
XLA Modules:
  0.0 613.8 jit_solution(8954921210702635121)
XLA Ops:
  8.0 0.0 all-gather.19.cloned.1.call-start
  8.0 11.2 %fusion.21 = f32[16,128,128]{2,1,0:T(8,128)} fusion(f32[512,2048]{1,0:T(8,128)} %param.14, f32[512,2048]{1,0:T(8,128)} %param.13), kind=kOutput, calls=%fused_computation.27 | convolution fusion | flops 1610612736 | bytes 9437184 | tf_op jit(solution)/shard_map/thd,the->hde/dot_general | solution.py:47
  19.2 5.1 copy.46
  24.3 5.7 copy.27
  30.1 9.2 %fusion.16 = f32[16,128,128]{2,1,0:T(8,128)} fusion(f32[512,16,128]{0,2,1:T(8,128)} %copy.27, f32[512,2048]{1,0:T(8,128)} %param.12), kind=kOutput, calls=%fused_computation.22 | convolution fusion | flops 1610612736 | bytes 9437184 | tf_op jit(solution)/shard_map/the,thd->hed/dot_general | solution.py:48
  39.3 94.8 %all-gather.19.cloned.1.call-done = f32[256,128,128]{2,1,0:T(8,128)} async-done(((f32[16,128,128]{2,1,0:T(8,128)}), f32[256,128,128]{2,1,0:T(8,128)}) %all-gather.19.cloned.1.call-update) | async-done | bytes 16777232 | tf_op jit(solution)/shard_map/all_gather | solution.py:10
  134.0 0.7 all-reduce.8.cloned.1.call-update
  134.8 0.0 all-gather.15.cloned.1.call-start
  134.8 93.1 %all-reduce.8.cloned.1.call-done = (f32[16,128,128]{2,1,0:T(8,128)}, f32[16,128,128]{2,1,0:T(8,128)}) async-done(((f32[16,128,128]{2,1,0:T(8,128)}, f32[16,128,128]{2,1,0:T(8,128)}), (f32[16,128,128]{2,1,0:T(8,128)}, f32[16,128,128]{2,1,0:T(8,128)})) %all-reduce.8.cloned.1.call-update) | async-done | bytes 2097168 | tf_op jit(solution)/shard_map/psum | solution.py:28
  228.0 0.0 all-gather.17.cloned.1.call-start
  228.0 0.5 all-gather.17.cloned.1.call-update
  228.5 15.4 %all-gather.15.cloned.1.call-done = f32[32,128,128]{2,1,0:T(8,128)} async-done(((f32[16,128,128]{2,1,0:T(8,128)}), f32[32,128,128]{2,1,0:T(8,128)}) %all-gather.15.cloned.1.call-update) | async-done | bytes 2097168 | tf_op jit(solution)/shard_map/all_gather | solution.py:10
  243.9 16.3 %all-gather.17.cloned.1.call-done = f32[32,128,128]{2,1,0:T(8,128)} async-done(((f32[16,128,128]{2,1,0:T(8,128)}), f32[32,128,128]{2,1,0:T(8,128)}) %all-gather.17.cloned.1.call-update) | async-done | bytes 2097168 | tf_op jit(solution)/shard_map/all_gather | solution.py:10
  260.2 0.6 all-reduce.10.cloned.1.call-update
  260.8 0.0 all-gather.21.cloned.1.call-start
  260.8 0.5 all-gather.21.cloned.1.call-update
  261.4 30.2 %all-reduce.10.cloned.1.call-done = (f32[1,16,128,128]{3,2,1,0:T(8,128)}, f32[1,16,128,128]{3,2,1,0:T(8,128)}) async-done(((f32[1,16,128,128]{3,2,1,0:T(8,128)}, f32[1,16,128,128]{3,2,1,0:T(8,128)}), (f32[1,16,128,128]{3,2,1,0:T(8,128)}, f32[1,16,128,128]{3,2,1,0:T(8,128)})) %all-reduce.10.cloned.1.call-update) | async-done | bytes 2097168 | tf_op jit(solution)/shard_map/psum | solution.py:30
  291.6 0.0 all-gather.13.cloned.1.call-start
  291.6 0.7 all-gather.13.cloned.1.call-update
  292.3 0.0 all-reduce.6.cloned.1.call-start
  292.4 0.5 all-reduce.6.cloned.1.call-update
  292.9 0.1 fusion.55
  293.1 19.5 %fusion.14 = f32[16,512,512]{2,1,0:T(8,128)} fusion(f32[512,2048]{1,0:T(8,128)} %param.12, f32[512,2048]{1,0:T(8,128)} %param.13), kind=kOutput, calls=%fused_computation.20 | convolution fusion | flops 6442450944 | bytes 25165824 | tf_op jit(solution)/shard_map/thd,shd->hts/dot_general | solution.py:58
  312.6 14.5 %fusion.11 = f32[16,512,512]{2,1,0:T(8,128)S(1)} fusion(f32[512,2048]{1,0:T(8,128)S(1)} %copy-done.4, f32[512,2048]{1,0:T(8,128)S(1)} %copy-done.5), kind=kOutput, calls=%fused_computation.17 | convolution fusion | flops 6442450944 | bytes 25165824 | tf_op jit(solution)/shard_map/the,she->hts/dot_general | solution.py:57
  327.1 14.5 %fusion.2 = f32[16,512,128]{1,2,0:T(8,128)} fusion(f32[16,512,512]{2,1,0:T(8,128)S(1)} %fusion.11, f32[512,512]{1,0:T(8,128)S(1)} %fusion.55, f32[512,2048]{1,0:T(8,128)} %param.12), kind=kOutput, calls=%fused_computation.8 | convolution fusion | flops 6446645248 | bytes 26214400 | tf_op jit(solution)/shard_map/hts,thd->shd/dot_general | solution.py:65
  341.6 21.3 %fusion.4 = f32[16,512,128]{1,2,0:T(8,128)} fusion(f32[16,512,512]{2,1,0:T(8,128)S(1)} %fusion.11, f32[512,512]{1,0:T(8,128)S(1)} %fusion.55, f32[512,2048]{1,0:T(8,128)} %param.13), kind=kOutput, calls=%fused_computation.10 | convolution fusion | flops 6446645248 | bytes 26214400 | tf_op jit(solution)/shard_map/hts,shd->thd/dot_general | solution.py:61
  362.9 44.5 %all-gather.21.cloned.1.call-done = f32[256,128,128]{2,1,0:T(8,128)} async-done(((f32[16,128,128]{2,1,0:T(8,128)}), f32[256,128,128]{2,1,0:T(8,128)}) %all-gather.21.cloned.1.call-update) | async-done | bytes 16777232 | tf_op jit(solution)/shard_map/all_gather | solution.py:10
  407.4 0.1 broadcast.6.clone
  407.5 0.1 broadcast.6.clone.1
  407.6 1.0 copy-done.1
  408.6 0.1 broadcast.6.clone.4
  408.7 0.1 broadcast.6.clone.5
  408.8 2.1 while.37
  408.8 2.1 bitcast_add_fusion.13
  410.9 45.8 %all-gather.11.cloned.1.call-done = f32[4,16,128,128]{3,2,1,0:T(8,128)} async-done(((f32[1,16,128,128]{3,2,1,0:T(8,128)}), f32[4,16,128,128]{3,2,1,0:T(8,128)}) %all-gather.11.cloned.1.call-update) | async-done | bytes 4194320 | tf_op jit(solution)/shard_map/all_gather | solution.py:10
  456.7 50.5 %all-gather.13.cloned.1.call-done = f32[4,16,128,128]{3,2,1,0:T(8,128)} async-done(((f32[1,16,128,128]{3,2,1,0:T(8,128)}), f32[4,16,128,128]{3,2,1,0:T(8,128)}) %all-gather.13.cloned.1.call-update) | async-done | bytes 4194320 | tf_op jit(solution)/shard_map/all_gather | solution.py:10
  507.2 0.1 broadcast.6.clone.2
  507.3 1.1 broadcast.6.clone.3
  508.4 44.6 %all-reduce.6.cloned.1.call-done = f32[16,128,128]{2,1,0:T(8,128)} async-done(((f32[16,128,128]{2,1,0:T(8,128)}), f32[16,128,128]{2,1,0:T(8,128)}) %all-reduce.6.cloned.1.call-update) | async-done | bytes 1048592 | tf_op jit(solution)/shard_map/psum | solution.py:50
  552.9 3.5 subtract_add_fusion
  556.4 1.0 copy-done.8
  557.5 3.8 fusion.23
  561.3 14.6 %fusion.29 = bf16[512,16,128]{0,2,1:T(8,128)(2,1)} fusion(f32[16,128,512]{2,1,0:T(8,128)S(1)} %fusion.23, f32[512,16,128]{0,2,1:T(8,128)S(1)} %copy-done.3, f32[16,512,512]{2,1,0:T(8,128)} %fusion.14, f32[512,512]{1,0:T(8,128)S(1)} %copy-done.7), kind=kOutput, calls=%fused_computation.36 | convolution fusion | flops 6449790976 | bytes 28311552 | tf_op jit(solution)/shard_map/hts,the->she/dot_general | solution.py:69
  575.9 3.9 copy.40
  579.8 9.2 %fusion.31 = bf16[512,16,128]{0,2,1:T(8,128)(2,1)} fusion(f32[16,512,128]{1,2,0:T(8,128)} %fusion.2, f32[16,128,128]{2,1,0:T(8,128)} %copy-done.8, f32[512,2048]{1,0:T(8,128)} %param.14), kind=kOutput, calls=%fused_computation.39 | convolution fusion | flops 1613758464 | bytes 11534336 | tf_op jit(solution)/shard_map/she,hed->shd/dot_general | solution.py:64
  589.0 4.1 copy.39
  593.1 9.2 %fusion.33 = bf16[512,16,128]{0,2,1:T(8,128)(2,1)} fusion(f32[16,512,128]{1,2,0:T(8,128)} %fusion.4, f32[16,128,128]{2,1,0:T(8,128)} %param.16, f32[16,128,128]{2,1,0:T(8,128)S(1)} %get-tuple-element.107, f32[16,128,128]{2,1,0:T(8,128)S(1)} %get-tuple-element.105, f32[16,128,128]{2,1,0:T(8,128)S(1)} %get-tuple-element.106, f32[512,2048]{1,0:T(8,128)} %param.15), kind=kOutput, calls=%fused_computation.42 | convolution fusion | flops 1614544896 | bytes 14680064 | tf_op jit(solution)/shard_map/the,hde->thd/dot_general | solution.py:60
  602.3 3.9 copy.38
  (24 shorter events, 0.1 us)
Async XLA Ops:
  8.0 126.0 %all-gather.19.cloned.1.call-start = ((), (), s32[]{:S(2)}) async-start(), calls=%async_computation.5 | async-start | bytes 17825792 | tf_op jit(solution)/shard_map/all_gather | solution.py:10
  134.0 93.9 %all-reduce.8.cloned.1.call-start = ((), (), s32[]{:S(2)}) async-start(), calls=%async_computation.7 | async-start | bytes 4194304 | tf_op jit(solution)/shard_map/psum | solution.py:28
  134.8 109.2 %all-gather.15.cloned.1.call-start = ((), (), s32[]{:S(2)}) async-start(), calls=%async_computation.3 | async-start | bytes 3145728 | tf_op jit(solution)/shard_map/all_gather | solution.py:10
  228.0 32.2 %all-gather.17.cloned.1.call-start = ((), (), s32[]{:S(2)}) async-start(), calls=%async_computation.4 | async-start | bytes 3145728 | tf_op jit(solution)/shard_map/all_gather | solution.py:10
  260.2 31.4 %all-reduce.10.cloned.1.call-start = ((), (), s32[]{:S(2)}) async-start(), calls=%async_computation.8 | async-start | bytes 4194304 | tf_op jit(solution)/shard_map/psum | solution.py:30
  260.8 146.6 %all-gather.21.cloned.1.call-start = ((), (), s32[]{:S(2)}) async-start(), calls=%async_computation.6 | async-start | bytes 17825792 | tf_op jit(solution)/shard_map/all_gather | solution.py:10
  261.4 195.3 %all-gather.11.cloned.1.call-start = ((), (), s32[]{:S(2)}) async-start(), calls=%async_computation | async-start | bytes 5242880 | tf_op jit(solution)/shard_map/all_gather | solution.py:10
  291.6 215.6 %all-gather.13.cloned.1.call-start = ((), (), s32[]{:S(2)}) async-start(), calls=%async_computation.1 | async-start | bytes 5242880 | tf_op jit(solution)/shard_map/all_gather | solution.py:10
  292.3 260.6 %all-reduce.6.cloned.1.call-start = ((), (), s32[]{:S(2)}) async-start(), calls=%async_computation.2 | async-start | bytes 2097152 | tf_op jit(solution)/shard_map/psum | solution.py:50
  293.0 48.6 %copy-start.6 = (f32[512,512]{1,0:T(8,128)}, f32[512,512]{1,0:T(8,128)S(1)}, u32[]{:S(2)}) copy-start(f32[512,512]{1,0:T(8,128)S(1)} %fusion.55) | copy-start | bytes 3145732
  293.1 19.6 %copy-start.4 = (f32[512,2048]{1,0:T(8,128)S(1)}, f32[512,2048]{1,0:T(8,128)}, u32[]{:S(2)}) copy-start(f32[512,2048]{1,0:T(8,128)} %param.15) | copy-start | bytes 12582916
  293.1 19.6 %copy-start.5 = (f32[512,2048]{1,0:T(8,128)S(1)}, f32[512,2048]{1,0:T(8,128)}, u32[]{:S(2)}) copy-start(f32[512,2048]{1,0:T(8,128)} %param.14) | copy-start | bytes 12582916
  407.6 1.0 copy-start.1
  410.9 45.8 %copy-start.2 = (f32[16,128,128]{2,1,0:T(8,128)}, f32[16,128,128]{2,1,0:T(8,128)S(1)}, u32[]{:S(2)}) copy-start(f32[16,128,128]{2,1,0:T(8,128)S(1)} %get-tuple-element.109) | copy-start | bytes 3145732
  552.9 4.5 copy-start
  556.4 1.0 copy-start.8
  557.5 3.8 copy-start.3
  557.5 3.8 copy-start.7
Sparse Core Ops, SparseCore 0:
  19.4 114.6 all-gather.18
  138.8 89.0 all-reduce.7
  229.7 14.2 all-gather.14
  245.5 14.6 all-gather.16
  263.4 28.1 all-reduce.9
  294.1 113.1 all-gather.20
  409.0 47.6 all-gather.10
  458.3 48.7 all-gather.12
Sparse Core Ops, SparseCore 1:
  298.2 254.7 all-reduce.5
where the time goes:
time: 621 us; the launch traced here: 614 us
  waiting for transfers between devices  439 us (71%)
  matrix products  127 us (20%)
  local copies, waits for them, and re-layouts  26.3 us (4%)
  between operations  16 us (3%)
    all_gather x6, waiting for transfers between devices, entering(): gathered = jax.tree.map(lambda a: lax.all_gather(a, axis), part)  267 us
    psum x1, waiting for transfers between devices, run_chain(): group_sum = lax.psum((local_terms[0], local_terms[1]), 'sc')  93.1 us
    psum x1, waiting for transfers between devices, shards(): total_grad = lax.psum(grad_local, ('sa', 'sb', 'sc'))  44.6 us
    psum x1, waiting for transfers between devices, run_chain(): block_sum = lax.psum((group_sum[0], group_sum[1]), 'sb')  30.2 us
    dot_general x1, matrix products, shards(): jnp.einsum('hts,shd->thd', grad_scores, key_t, precision=highest)  21.3 us
    dot_general x1, matrix products, shards(): jnp.einsum('thd,shd->hts', query_t, key_t, precision=highest) * lower  19.5 us
    unnamed x22, local copies, waits for them, and re-layouts  19 us
    dot_general x1, matrix products, shards(): jnp.einsum('hts,the->she', attn_scores, grad_t, precision=highest)  14.6 us
  transfers between devices with their start and end apart: 9, of which 9 were waited for; matrix products, arithmetic and copies ran while one was open for 15% of the time, Pallas kernels for 0%

commit v1 on v0

--- a/solution.py
+++ b/solution.py
@@ -47,7 +47,8 @@
     kv_local = jnp.einsum("thd,the->hde", key_t, value_t, precision=highest)
     grad_local = jnp.einsum("the,thd->hed", grad_t, query_t, precision=highest)
     prior_kv, prior_grad = run_chain((kv_local, grad_local))
-    total_grad = lax.psum(grad_local, ("sa", "sb", "sc"))
+    parts = lax.all_gather(grad_local, ("sa", "sb", "sc"), axis=0, tiled=False)
+    total_grad = parts.sum(axis=0)
     state_before = prefix_state + prior_kv
     state_after = suffix_state + (total_grad - prior_grad - grad_local)
     lower = (

time: 621 us -> 882 us (1.42)
  waiting for transfers between devices: 439 us -> 667 us
  other arithmetic: 5.71 us -> 46.3 us
    all_gather x0 -> x1, waiting for transfers between devices: none -> 274 us  [shards(): parts = lax.all_gather(grad_local, ('sa', 'sb', 'sc'), axis=0, tiled=False)]
    psum x1 -> x0, waiting for transfers between devices: 44.6 us -> none  [shards(): total_grad = lax.psum(grad_local, ('sa', 'sb', 'sc'))]
    reduce_sum x0 -> x1, other arithmetic: none -> 41.5 us  [shards(): total_grad = parts.sum(axis=0)]
    unnamed x22 -> x30, local copies, waits for them, and re-layouts: 19 us -> 16.2 us
  transfers between devices with their start and end apart: 9 -> 9, of which waited for: 9 -> 9; matrix products, arithmetic and copies ran while one was open for 15% -> 12% of each run, Pallas kernels for 0% -> 0%
where the time goes in v1:
time: 882 us; the launch traced here: 875 us
  waiting for transfers between devices  667 us (76%)
  matrix products  124 us (14%)
  other arithmetic  46.3 us (5%)
  local copies, waits for them, and re-layouts  23.5 us (3%)
  between operations  14.3 us (2%)
    all_gather x1, waiting for transfers between devices, shards(): parts = lax.all_gather(grad_local, ('sa', 'sb', 'sc'), axis=0, tiled=False)  274 us
    all_gather x6, waiting for transfers between devices, entering(): gathered = jax.tree.map(lambda a: lax.all_gather(a, axis), part)  266 us
    psum x1, waiting for transfers between devices, run_chain(): group_sum = lax.psum((local_terms[0], local_terms[1]), 'sc')  93.1 us
    reduce_sum x1, other arithmetic, shards(): total_grad = parts.sum(axis=0)  41.5 us
    psum x1, waiting for transfers between devices, run_chain(): block_sum = lax.psum((group_sum[0], group_sum[1]), 'sb')  30.2 us
    dot_general x1, matrix products, shards(): jnp.einsum('hts,shd->thd', grad_scores, key_t, precision=highest)  20.9 us
    dot_general x1, matrix products, shards(): jnp.einsum('thd,shd->hts', query_t, key_t, precision=highest) * lower  19.5 us
  transfers between devices with their start and end apart: 9, of which 9 were waited for; matrix products, arithmetic and copies ran while one was open for 12% of the time, Pallas kernels for 0%

profile of v1, /device:TPU:1, one launch (start us, length us, event | category | flops | bytes accessed | tf_op | source)
XLA Modules:
  0.0 875.2 jit_solution(5194552236594441276)
XLA Ops:
  7.2 0.0 all-gather.21.cloned.1.call-start
  7.2 11.2 %fusion.21 = f32[16,128,128]{2,1,0:T(8,128)} fusion(f32[512,2048]{1,0:T(8,128)} %param.14, f32[512,2048]{1,0:T(8,128)} %param.13), kind=kOutput, calls=%fused_computation.27 | convolution fusion | flops 1610612736 | bytes 9437184 | tf_op jit(solution)/shard_map/thd,the->hde/dot_general | solution.py:47
  18.4 5.2 copy.46
  23.6 5.8 copy.27
  29.3 9.2 %fusion.16 = f32[16,128,128]{2,1,0:T(8,128)} fusion(f32[512,16,128]{0,2,1:T(8,128)} %copy.27, f32[512,2048]{1,0:T(8,128)} %param.12), kind=kOutput, calls=%fused_computation.22 | convolution fusion | flops 1610612736 | bytes 9437184 | tf_op jit(solution)/shard_map/the,thd->hed/dot_general | solution.py:48
  38.6 94.6 %all-gather.21.cloned.1.call-done = f32[256,128,128]{2,1,0:T(8,128)} async-done(((f32[16,128,128]{2,1,0:T(8,128)}), f32[256,128,128]{2,1,0:T(8,128)}) %all-gather.21.cloned.1.call-update) | async-done | bytes 16777232 | tf_op jit(solution)/shard_map/all_gather | solution.py:10
  133.2 0.7 all-reduce.5.cloned.1.call-update
  133.9 0.0 all-gather.17.cloned.1.call-start
  134.0 93.1 %all-reduce.5.cloned.1.call-done = (f32[16,128,128]{2,1,0:T(8,128)}, f32[16,128,128]{2,1,0:T(8,128)}) async-done(((f32[16,128,128]{2,1,0:T(8,128)}, f32[16,128,128]{2,1,0:T(8,128)}), (f32[16,128,128]{2,1,0:T(8,128)}, f32[16,128,128]{2,1,0:T(8,128)})) %all-reduce.5.cloned.1.call-update) | async-done | bytes 2097168 | tf_op jit(solution)/shard_map/psum | solution.py:28
  227.1 0.0 all-gather.19.cloned.1.call-start
  227.2 0.5 all-gather.19.cloned.1.call-update
  227.7 15.4 %all-gather.17.cloned.1.call-done = f32[32,128,128]{2,1,0:T(8,128)} async-done(((f32[16,128,128]{2,1,0:T(8,128)}), f32[32,128,128]{2,1,0:T(8,128)}) %all-gather.17.cloned.1.call-update) | async-done | bytes 2097168 | tf_op jit(solution)/shard_map/all_gather | solution.py:10
  243.1 16.3 %all-gather.19.cloned.1.call-done = f32[32,128,128]{2,1,0:T(8,128)} async-done(((f32[16,128,128]{2,1,0:T(8,128)}), f32[32,128,128]{2,1,0:T(8,128)}) %all-gather.19.cloned.1.call-update) | async-done | bytes 2097168 | tf_op jit(solution)/shard_map/all_gather | solution.py:10
  259.4 0.6 all-reduce.7.cloned.1.call-update
  259.9 0.0 all-gather.23.cloned.1.call-start
  260.0 0.5 all-gather.23.cloned.1.call-update
  260.6 30.2 %all-reduce.7.cloned.1.call-done = (f32[1,16,128,128]{3,2,1,0:T(8,128)}, f32[1,16,128,128]{3,2,1,0:T(8,128)}) async-done(((f32[1,16,128,128]{3,2,1,0:T(8,128)}, f32[1,16,128,128]{3,2,1,0:T(8,128)}), (f32[1,16,128,128]{3,2,1,0:T(8,128)}, f32[1,16,128,128]{3,2,1,0:T(8,128)})) %all-reduce.7.cloned.1.call-update) | async-done | bytes 2097168 | tf_op jit(solution)/shard_map/psum | solution.py:30
  290.8 0.7 all-gather.15.cloned.1.call-update
  291.5 0.0 all-gather.25.cloned.1.call-start
  291.6 0.7 all-gather.25.cloned.1.call-update
  292.3 0.1 fusion.55
  292.4 19.5 %fusion.14 = f32[16,512,512]{2,1,0:T(8,128)} fusion(f32[512,2048]{1,0:T(8,128)} %param.12, f32[512,2048]{1,0:T(8,128)} %param.13), kind=kOutput, calls=%fused_computation.20 | convolution fusion | flops 6442450944 | bytes 25165824 | tf_op jit(solution)/shard_map/thd,shd->hts/dot_general | solution.py:59
  312.0 14.5 %fusion.11 = f32[16,512,512]{2,1,0:T(8,128)S(1)} fusion(f32[512,2048]{1,0:T(8,128)S(1)} %copy-done.7, f32[512,2048]{1,0:T(8,128)S(1)} %copy-done.8), kind=kOutput, calls=%fused_computation.17 | convolution fusion | flops 6442450944 | bytes 25165824 | tf_op jit(solution)/shard_map/the,she->hts/dot_general | solution.py:58
  326.4 20.9 %fusion.4 = f32[16,512,128]{1,2,0:T(8,128)} fusion(f32[16,512,512]{2,1,0:T(8,128)S(1)} %fusion.11, f32[512,512]{1,0:T(8,128)S(1)} %fusion.55, f32[512,2048]{1,0:T(8,128)} %param.13), kind=kOutput, calls=%fused_computation.10 | convolution fusion | flops 6446645248 | bytes 26214400 | tf_op jit(solution)/shard_map/hts,shd->thd/dot_general | solution.py:62
  347.3 14.9 %fusion.2 = f32[16,512,128]{1,2,0:T(8,128)} fusion(f32[16,512,512]{2,1,0:T(8,128)S(1)} %fusion.11, f32[512,512]{1,0:T(8,128)S(1)} %fusion.55, f32[512,2048]{1,0:T(8,128)} %param.12), kind=kOutput, calls=%fused_computation.8 | convolution fusion | flops 6446645248 | bytes 26214400 | tf_op jit(solution)/shard_map/hts,thd->shd/dot_general | solution.py:66
  362.2 43.5 %all-gather.23.cloned.1.call-done = f32[256,128,128]{2,1,0:T(8,128)} async-done(((f32[16,128,128]{2,1,0:T(8,128)}), f32[256,128,128]{2,1,0:T(8,128)}) %all-gather.23.cloned.1.call-update) | async-done | bytes 16777232 | tf_op jit(solution)/shard_map/all_gather | solution.py:10
  405.7 0.1 broadcast.6.clone
  405.8 0.1 broadcast.6.clone.1
  405.9 1.0 copy-done.1
  406.9 0.1 broadcast.6.clone.4
  407.0 0.1 broadcast.6.clone.5
  407.1 2.1 while.37
  407.1 2.1 bitcast_add_fusion.13
  409.2 46.0 %all-gather.13.cloned.1.call-done = f32[4,16,128,128]{3,2,1,0:T(8,128)} async-done(((f32[1,16,128,128]{3,2,1,0:T(8,128)}), f32[4,16,128,128]{3,2,1,0:T(8,128)}) %all-gather.13.cloned.1.call-update) | async-done | bytes 4194320 | tf_op jit(solution)/shard_map/all_gather | solution.py:10
  455.2 50.3 %all-gather.15.cloned.1.call-done = f32[4,16,128,128]{3,2,1,0:T(8,128)} async-done(((f32[1,16,128,128]{3,2,1,0:T(8,128)}), f32[4,16,128,128]{3,2,1,0:T(8,128)}) %all-gather.15.cloned.1.call-update) | async-done | bytes 4194320 | tf_op jit(solution)/shard_map/all_gather | solution.py:10
  505.5 0.1 broadcast.6.clone.2
  505.6 1.1 broadcast.6.clone.3
  506.7 9.1 %fusion.33 = bf16[512,16,128]{0,2,1:T(8,128)(2,1)} fusion(f32[16,512,128]{1,2,0:T(8,128)} %fusion.4, f32[16,128,128]{2,1,0:T(8,128)} %param.16, f32[16,128,128]{2,1,0:T(8,128)S(1)} %get-tuple-element.107, f32[16,128,128]{2,1,0:T(8,128)S(1)} %get-tuple-element.105, f32[16,128,128]{2,1,0:T(8,128)S(1)} %get-tuple-element.106, f32[512,2048]{1,0:T(8,128)} %param.15), kind=kOutput, calls=%fused_computation.42 | convolution fusion | flops 1614544896 | bytes 14680064 | tf_op jit(solution)/shard_map/the,hde->thd/dot_general | solution.py:61
  515.8 4.1 copy.38
  519.9 273.6 %all-gather.25.cloned.1.call-done = f32[2048,128,128]{2,1,0:T(8,128)} async-done(((f32[16,128,128]{2,1,0:T(8,128)}), f32[2048,128,128]{2,1,0:T(8,128)}) %all-gather.25.cloned.1.call-update) | async-done | bytes 134217744 | tf_op jit(solution)/shard_map/all_gather | solution.py:50
  793.5 41.5 %reduce_sum.9 = f32[16,128,128]{2,1,0:T(8,128)} reduce(f32[128,16,128,128]{3,2,1,0:T(8,128)} %bitcast.15, f32[]{:T(128)} %constant.45.clone.1), dimensions={0}, to_apply=%region_10.11 | reduce | flops 33292288 | bytes 135266304 | tf_op jit(solution)/shard_map/reduce_sum | solution.py:51
  835.0 2.5 subtract_add_fusion
  837.6 1.0 copy-done.11
  838.6 3.8 fusion.23
  842.4 13.5 %fusion.29 = bf16[512,16,128]{0,2,1:T(8,128)(2,1)S(1)} fusion(f32[16,128,512]{2,1,0:T(8,128)S(1)} %fusion.23, f32[512,16,128]{0,2,1:T(8,128)S(1)} %copy-done.6, f32[16,512,512]{2,1,0:T(8,128)} %fusion.14, f32[512,512]{1,0:T(8,128)S(1)} %copy-done.10), kind=kOutput, calls=%fused_computation.36 | convolution fusion | flops 6449790976 | bytes 28311552 | tf_op jit(solution)/shard_map/hts,the->she/dot_general | solution.py:70
  855.9 2.6 copy.40
  858.5 7.6 fusion.31
  866.0 2.4 copy.39
  (33 shorter events, 0.2 us)
Async XLA Ops:
  7.2 126.0 %all-gather.21.cloned.1.call-start = ((), (), s32[]{:S(2)}) async-start(), calls=%async_computation.4 | async-start | bytes 17825792 | tf_op jit(solution)/shard_map/all_gather | solution.py:10
  133.2 93.9 %all-reduce.5.cloned.1.call-start = ((), (), s32[]{:S(2)}) async-start(), calls=%async_computation.7 | async-start | bytes 4194304 | tf_op jit(solution)/shard_map/psum | solution.py:28
  133.9 109.2 %all-gather.17.cloned.1.call-start = ((), (), s32[]{:S(2)}) async-start(), calls=%async_computation.2 | async-start | bytes 3145728 | tf_op jit(solution)/shard_map/all_gather | solution.py:10
  227.1 32.2 %all-gather.19.cloned.1.call-start = ((), (), s32[]{:S(2)}) async-start(), calls=%async_computation.3 | async-start | bytes 3145728 | tf_op jit(solution)/shard_map/all_gather | solution.py:10
  259.4 31.4 %all-reduce.7.cloned.1.call-start = ((), (), s32[]{:S(2)}) async-start(), calls=%async_computation.8 | async-start | bytes 4194304 | tf_op jit(solution)/shard_map/psum | solution.py:30
  259.9 145.7 %all-gather.23.cloned.1.call-start = ((), (), s32[]{:S(2)}) async-start(), calls=%async_computation.5 | async-start | bytes 17825792 | tf_op jit(solution)/shard_map/all_gather | solution.py:10
  260.5 194.7 %all-gather.13.cloned.1.call-start = ((), (), s32[]{:S(2)}) async-start(), calls=%async_computation | async-start | bytes 5242880 | tf_op jit(solution)/shard_map/all_gather | solution.py:10
  290.8 214.7 %all-gather.15.cloned.1.call-start = ((), (), s32[]{:S(2)}) async-start(), calls=%async_computation.1 | async-start | bytes 5242880 | tf_op jit(solution)/shard_map/all_gather | solution.py:10
  291.5 502.0 %all-gather.25.cloned.1.call-start = ((), (), s32[]{:S(2)}) async-start(), calls=%async_computation.6 | async-start | bytes 135266304 | tf_op jit(solution)/shard_map/all_gather | solution.py:50
  292.4 54.9 %copy-start.9 = (f32[512,512]{1,0:T(8,128)}, f32[512,512]{1,0:T(8,128)S(1)}, u32[]{:S(2)}) copy-start(f32[512,512]{1,0:T(8,128)S(1)} %fusion.55) | copy-start | bytes 3145732
  292.4 19.6 %copy-start.7 = (f32[512,2048]{1,0:T(8,128)S(1)}, f32[512,2048]{1,0:T(8,128)}, u32[]{:S(2)}) copy-start(f32[512,2048]{1,0:T(8,128)} %param.15) | copy-start | bytes 12582916
  292.4 19.6 %copy-start.8 = (f32[512,2048]{1,0:T(8,128)S(1)}, f32[512,2048]{1,0:T(8,128)}, u32[]{:S(2)}) copy-start(f32[512,2048]{1,0:T(8,128)} %param.14) | copy-start | bytes 12582916
  405.9 1.0 copy-start.1
  409.2 46.0 %copy-start.3 = (f32[16,128,128]{2,1,0:T(8,128)}, f32[16,128,128]{2,1,0:T(8,128)S(1)}, u32[]{:S(2)}) copy-start(f32[16,128,128]{2,1,0:T(8,128)S(1)} %get-tuple-element.109) | copy-start | bytes 3145732
  793.5 41.5 %copy-start.2 = (f32[16,128,128]{2,1,0:T(8,128)S(1)}, f32[16,128,128]{2,1,0:T(8,128)}, u32[]{:S(2)}) copy-start(f32[16,128,128]{2,1,0:T(8,128)} %copy-done.1) | copy-start | bytes 3145732
  793.5 41.5 %copy-start.4 = (f32[16,128,128]{2,1,0:T(8,128)S(1)}, f32[16,128,128]{2,1,0:T(8,128)}, u32[]{:S(2)}) copy-start(f32[16,128,128]{2,1,0:T(8,128)} %copy-done.3) | copy-start | bytes 3145732
  793.5 41.5 %copy-start.5 = (f32[16,128,128]{2,1,0:T(8,128)S(1)}, f32[16,128,128]{2,1,0:T(8,128)}, u32[]{:S(2)}) copy-start(f32[16,128,128]{2,1,0:T(8,128)} %get-tuple-element.108) | copy-start | bytes 3145732
  835.0 3.5 copy-start
  837.6 1.0 copy-start.11
  838.6 3.8 copy-start.6
  838.6 3.8 copy-start.10
  855.9 2.6 copy-start.12
Sparse Core Ops, SparseCore 0:
  18.5 114.6 all-gather.20
  138.0 89.0 all-reduce.4
  228.9 14.2 all-gather.16
  244.7 14.6 all-gather.18
  262.5 28.1 all-reduce.6
  293.3 112.3 all-gather.22
  407.3 47.8 all-gather.12
  456.9 48.5 all-gather.14
  509.2 284.1 all-gather.24
